TPU v7x, 32 devices: a whole 2x2x4 slice. The times are simulated.
32 devices in a mesh: context: 8 (over z, y), tensor: 4 (over x, core).
Axes of the slice: x: 2, y: 2, z: 4, core: 2. Of those that a mesh axis runs over, the one named last changes fastest.
Arguments:
- tokens: bfloat16 [4096, 4096], P(('context', 'tensor')), may hold values from -6 to 6
- norm_gain: float32 [4096], replicated, may hold values from 0.5 to 1.5
- in_weight: bfloat16 [4096, 3, 2048], P(None, None, 'tensor'), may hold values from -0.09375 to 0.09375
- short_weight: float32 [3, 3, 2048], P(None, None, 'tensor'), may hold values from -3 to 3
- long_filter: float32 [4096, 2048], P('context', 'tensor'), may hold values from -0.09375 to 0.09375
- skip_gain: float32 [2048], P('tensor'), may hold values from -4 to 4
Outputs:
- block_out: bfloat16 [4096, 2048], P('context', 'tensor')
All inputs are finite; a program needn't handle non-finite values.
Results may differ from a plain program's by a relative error of at most 0.0065.
Values may be sent and summed in bfloat16 or wider, within the bound.
No kernel may reach another device: no remote copies, remote signals or barrier semaphores. Data moves between devices by JAX's collectives and lax.ppermute only.
A program may use at most 128 MiB of HBM per device.

v0:
```python
import math
import jax
import jax.numpy as jnp
from jax import lax
from jax.sharding import PartitionSpec as P

eps = 1e-06


def shifted(x, axis, by):
    peers = lax.axis_size(axis)
    pairs = [(i, i + by) for i in range(peers) if 0 <= i + by < peers]
    return lax.ppermute(x, axis, pairs)


def along_rows(table, block):
    return jnp.einsum("kj,tjc->tkc", table, block, precision=lax.Precision.HIGHEST)


def transposed(stacked, forward):
    dev_count = lax.axis_size("context")
    planes, turn_count, length, channels = stacked.shape
    ranks = jnp.arange(dev_count, dtype=jnp.int32)
    phase_angle = (ranks[:, None] * ranks[None, :] % dev_count).astype(jnp.float32) * (
        2.0 * math.pi / dev_count
    )
    table_re = jnp.cos(phase_angle)
    if forward:
        table_im = -jnp.sin(phase_angle)
    else:
        table_im = jnp.sin(phase_angle)

    def combine_rows(received):
        rows_re = jnp.einsum(
            "fp,tpjc->tfjc", table_re, received[0], precision=lax.Precision.HIGHEST
        ) - jnp.einsum("fp,tpjc->tfjc", table_im, received[1], precision=lax.Precision.HIGHEST)
        rows_im = jnp.einsum(
            "fp,tpjc->tfjc", table_re, received[1], precision=lax.Precision.HIGHEST
        ) + jnp.einsum("fp,tpjc->tfjc", table_im, received[0], precision=lax.Precision.HIGHEST)
        return jnp.stack([rows_re, rows_im])

    sectioned = stacked.reshape(planes, turn_count, 1, length, channels)
    if forward:
        result_grid = lax.all_to_all(
            combine_rows(
                lax.all_to_all(sectioned, "context", split_axis=3, concat_axis=2, tiled=True)
            ),
            "context",
            split_axis=2,
            concat_axis=3,
            tiled=True,
        )
    else:
        result_grid = lax.all_to_all(
            combine_rows(
                lax.all_to_all(sectioned, "context", split_axis=3, concat_axis=2, tiled=True)
            ),
            "context",
            split_axis=2,
            concat_axis=3,
            tiled=True,
        )
    return result_grid.reshape(planes, turn_count, length, channels)


def local(tokens, norm_gain, in_weight, short_weight, long_filter, skip_gain):
    width = tokens.shape[1]
    channels = in_weight.shape[2]
    tap_count = short_weight.shape[0]
    flat_weight = in_weight.reshape(width, 3 * channels)
    values = lax.all_gather(tokens, "tensor", axis=0, tiled=True).astype(jnp.float32)
    inv_rms = lax.rsqrt(jnp.mean(values * values, axis=1, keepdims=True) + eps)
    normed = (values * inv_rms * norm_gain).astype(jnp.bfloat16)
    projected = jnp.dot(normed, flat_weight, preferred_element_type=jnp.float32)
    length = projected.shape[0]
    before = shifted(projected[length - (tap_count - 1) :], "context", 1)
    padded = jnp.concatenate([before, projected], axis=0)
    tap_rows = short_weight.reshape(tap_count, 3 * channels)
    mixed_rows = jnp.zeros_like(projected)
    for tap_index in range(tap_count):
        offset = tap_count - 1 - tap_index
        mixed_rows = mixed_rows + tap_rows[tap_index] * padded[offset : offset + length]
    query_part = mixed_rows[:, :channels]
    key_part = mixed_rows[:, channels : 2 * channels]
    value_part = mixed_rows[:, 2 * channels :]
    gated = key_part * value_part
    dev_count = lax.axis_size("context")
    device = lax.axis_index("context")
    total_points = 2 * dev_count * length
    half_turn = device.astype(jnp.float32) * (math.pi / dev_count)
    source = jnp.concatenate([gated, long_filter], axis=1)
    zero_plane = jnp.zeros_like(source)
    shifted_re = source * jnp.cos(half_turn)
    shifted_im = -source * jnp.sin(half_turn)
    stacked = jnp.stack([jnp.stack([source, shifted_re]), jnp.stack([zero_plane, shifted_im])])
    stacked = transposed(stacked, True)
    turn_ids = jnp.arange(2, dtype=jnp.int32)
    coarse = 2 * device + turn_ids
    positions = jnp.arange(length, dtype=jnp.int32)
    twist_phase = (positions[None, :] * coarse[:, None] % total_points).astype(jnp.float32) * (
        2.0 * math.pi / total_points
    )
    twist_re = jnp.cos(twist_phase)[:, :, None]
    twist_im = -jnp.sin(twist_phase)[:, :, None]
    turned_re = stacked[0] * twist_re - stacked[1] * twist_im
    turned_im = stacked[0] * twist_im + stacked[1] * twist_re
    table_phase = (positions[:, None] * positions[None, :] % length).astype(jnp.float32) * (
        2.0 * math.pi / length
    )
    cos_table = jnp.cos(table_phase)
    sin_table = jnp.sin(table_phase)
    spec_re = along_rows(cos_table, turned_re) + along_rows(sin_table, turned_im)
    spec_im = along_rows(cos_table, turned_im) - along_rows(sin_table, turned_re)
    signal_re = spec_re[:, :, :channels]
    signal_im = spec_im[:, :, :channels]
    filt_re = spec_re[:, :, channels:]
    filt_im = spec_im[:, :, channels:]
    prod_re = signal_re * filt_re - signal_im * filt_im
    prod_im = signal_re * filt_im + signal_im * filt_re
    back_re = along_rows(cos_table, prod_re) - along_rows(sin_table, prod_im)
    back_im = along_rows(sin_table, prod_re) + along_rows(cos_table, prod_im)
    untw_re = back_re * twist_re + back_im * twist_im
    untw_im = back_im * twist_re - back_re * twist_im
    stacked = jnp.stack([untw_re, untw_im])
    stacked = transposed(stacked, False)
    conv = (
        stacked[0, 0] + stacked[0, 1] * jnp.cos(half_turn) - stacked[1, 1] * jnp.sin(half_turn)
    ) / total_points
    block_out = query_part * (conv + skip_gain * gated)
    return block_out.astype(jnp.bfloat16)


def solution(mesh):
    return jax.shard_map(
        local,
        mesh=mesh,
        in_specs=(
            P(("context", "tensor"), None),
            P(),
            P(None, None, "tensor"),
            P(None, None, "tensor"),
            P("context", "tensor"),
            P("tensor"),
        ),
        out_specs=P("context", "tensor"),
        check_vma=False,
    )
```

profile of v0, /device:TPU:0, one launch (start us, length us, event | category | flops | bytes accessed | tf_op | source)
XLA Modules:
  0.0 858.5 jit_solution(13042086948463147038)
XLA Ops:
  7.3 17.1 %copy.52 = bf16[4096,3,512]{0,2,1:T(8,128)(2,1)} copy(bf16[4096,3,512]{2,0,1:T(8,128)(2,1)} %param.8) | data formatting | bytes 25165824 | tf_op args[2]
  24.3 21.8 %all-gather.2.cloned.1.call-done = bf16[512,4096]{1,0:T(8,128)(2,1)} async-done(((bf16[128,4096]{1,0:T(8,128)(2,1)}), bf16[512,4096]{1,0:T(8,128)(2,1)}) %all-gather.2.cloned.1.call-update) | async-done | bytes 4194320 | tf_op jit(solution)/shard_map/all_gather | solution.py:71
  49.6 9.4 %fusion.3 = f32[512,1536]{1,0:T(8,128)S(1)} fusion(bf16[4096,1536]{0,1:T(8,128)(2,1)} %bitcast.124, bf16[512,4096]{1,0:T(8,128)(2,1)S(1)} %copy-done.1, f32[4096]{0:T(1024)S(1)} %copy-done.6, f32[512]{0:T(512)S(1)} %add_rsqrt_fusion), kind=kOutput, calls=%fused_computation.7 | convolution fusion | flops 6450839552 | bytes 19941376 | tf_op jit(solution)/shard_map/dot_general | solution.py:74
  73.2 7.4 copy.53
  80.6 188.8 %all_to_all.16 = f32[2,2,1,512,1024]{4,1,0,2,3:T(2,128)} all-to-all(f32[2,2,1,512,1024]{4,1,0,2,3:T(2,128)S(1)} %copy.53), channel_id=1, replica_groups=mesh['context'=8,'tensor'=4] {'context'}, dimensions={3} | all-to-all | bytes 16777216 | tf_op jit(solution)/shard_map/all_to_all | solution.py:46
  269.4 9.6 %fusion.167 = (f32[1,2,1,512,1024]{4,1,0,2,3:T(2,128)}, f32[1,2,1,512,1024]{4,1,0,2,3:T(2,128)}) fusion(f32[2,2,1,512,1024]{4,1,0,2,3:T(2,128)} %all_to_all.16), kind=kLoop, calls=%fused_computation.185 | loop fusion | bytes 16777216 | tf_op jit(solution)/shard_map/slice | solution.py:35
  282.5 7.8 fusion.9
  290.3 8.1 fusion.7
  299.8 8.1 subtract_bitcast_fusion.1
  307.9 8.0 add_bitcast_fusion.1
  317.6 8.5 copy.60
  326.1 5.0 all-to-all-start.1
  331.2 181.8 %all-to-all-done.1 = f32[2,2,8,64,1024]{4,3,1,0,2:T(8,128)} async-done(((f32[2,2,8,64,1024]{4,3,1,0,2:T(8,128)}), f32[2,2,8,64,1024]{4,3,1,0,2:T(8,128)}, u32[]{:S(2)}, u32[]{:S(2)}) %all-to-all-start.1) | async-done | bytes 8388640 | tf_op jit(solution)/shard_map/all_to_all | solution.py:44
  518.3 18.1 %fusion.37 = f32[2,1024,512]{2,1,0:T(8,128)S(1)} fusion(f32[2,512,1024]{2,1,0:T(8,128)S(1)} %bitcast.111, f32[2,512,1024]{2,1,0:T(8,128)S(1)} %bitcast.107, f32[2,512]{1,0:T(2,128)S(1)} %get-tuple-element.21, f32[2,512]{1,0:T(2,128)S(1)} %get-tuple-element.20), kind=kOutput, calls=%fused_computation.59 | convolution fusion | flops 6449266688 | bytes 12591104 | tf_op jit(solution)/shard_map/kj,tjc->tkc/dot_general | solution.py:17
  536.4 18.5 %fusion.38 = f32[2,1024,512]{2,1,0:T(8,128)S(1)} fusion(f32[2,512,1024]{2,1,0:T(8,128)S(1)} %bitcast.112, f32[2,512,1024]{2,1,0:T(8,128)S(1)} %bitcast.108, f32[2,512]{1,0:T(2,128)S(1)} %get-tuple-element.21, f32[2,512]{1,0:T(2,128)S(1)} %get-tuple-element.20), kind=kOutput, calls=%fused_computation.60 | convolution fusion | flops 6449266688 | bytes 12591104 | tf_op jit(solution)/shard_map/kj,tjc->tkc/dot_general | solution.py:17
  554.9 18.2 %add_bitcast_fusion = f32[2,512,1024]{1,2,0:T(8,128)S(1)} fusion(f32[2,1024,512]{2,1,0:T(8,128)S(1)} %fusion.37, f32[2,512,1024]{2,1,0:T(8,128)S(1)} %bitcast.113, f32[2,512,1024]{2,1,0:T(8,128)S(1)} %bitcast.109, f32[2,512]{1,0:T(2,128)S(1)} %get-tuple-element.21, f32[2,512]{1,0:T(2,128)S(1)} %get-tuple-element.20), kind=kOutput, calls=%fused_computation.12 | convolution fusion | flops 6450315264 | bytes 16785408 | tf_op jit(solution)/shard_map/kj,tjc->tkc/dot_general | solution.py:17
  573.1 18.6 %subtract_bitcast_fusion = f32[2,512,1024]{1,2,0:T(8,128)S(1)} fusion(f32[2,1024,512]{2,1,0:T(8,128)S(1)} %fusion.38, f32[2,512,1024]{2,1,0:T(8,128)S(1)} %bitcast.114, f32[2,512,1024]{2,1,0:T(8,128)S(1)} %bitcast.110, f32[2,512]{1,0:T(2,128)S(1)} %get-tuple-element.21, f32[2,512]{1,0:T(2,128)S(1)} %get-tuple-element.20), kind=kOutput, calls=%fused_computation.11 | convolution fusion | flops 6450315264 | bytes 16785408 | tf_op jit(solution)/shard_map/kj,tjc->tkc/dot_general | solution.py:17
  593.1 8.4 fusion.49
  601.5 8.4 fusion.55
  609.9 8.6 %convolution_add_fusion = f32[2,512,512]{2,1,0:T(8,128)S(1)} fusion(f32[2,512,512]{2,1,0:T(8,128)S(1)} %fusion.49, f32[2,512,512]{1,2,0:T(8,128)S(1)} %get-tuple-element.5), kind=kOutput, calls=%fused_computation.54 | convolution fusion | flops 3225419776 | bytes 6291456 | tf_op jit(solution)/shard_map/kj,tjc->tkc/dot_general | solution.py:17
  618.6 8.7 %add_bitcast_fusion.3 = (f32[1,2,512,512]{2,3,1,0:T(8,128)S(1)}, f32[1,2,512,512]{2,3,1,0:T(8,128)S(1)}) fusion(f32[2,512,512]{2,1,0:T(8,128)S(1)} %convolution_add_fusion, f32[2,512]{1,0:T(2,128)S(1)} %get-tuple-element.21, f32[2,512]{1,0:T(2,128)S(1)} %get-tuple-element.20, f32[2,512,512]{2,1,0:T(8,128)S(1)} %fusion.55, ...), kind=kOutput, calls=%fused_computation.41 | convolution fusion | flops 3228565504 | bytes 10493952 | tf_op jit(solution)/shard_map/kj,tjc->tkc/dot_general | solution.py:17
  629.7 7.3 copy.67
  637.0 96.9 %all_to_all.17 = f32[2,2,1,512,512]{4,1,0,2,3:T(2,128)S(1)} all-to-all(f32[2,2,1,512,512]{4,1,0,2,3:T(2,128)} %copy.67), channel_id=1, replica_groups=mesh['context'=8,'tensor'=4] {'context'}, dimensions={3} | all-to-all | bytes 8388608 | tf_op jit(solution)/shard_map/all_to_all | solution.py:56
  752.5 96.5 %all_to_all.18 = f32[2,2,8,64,512]{4,3,1,0,2:T(8,128)S(1)} all-to-all(f32[2,2,8,64,512]{4,3,1,0,2:T(8,128)S(1)} %copy.74), channel_id=1, replica_groups=mesh['context'=8,'tensor'=4] {'context'}, dimensions={2} | all-to-all | bytes 8388608 | tf_op jit(solution)/shard_map/all_to_all | solution.py:54
  (53 shorter events, 54.6 us)
Async XLA Ops:
  6.5 39.6 %all-gather.2.cloned.1.call-start = ((), (), s32[]{:S(2)}) async-start(), calls=%async_computation.4 | async-start | bytes 5242880 | tf_op jit(solution)/shard_map/all_gather | solution.py:71
  7.3 42.1 %copy-start.6 = (f32[4096]{0:T(1024)S(1)}, f32[4096]{0:T(1024)}, u32[]{:S(2)}) copy-start(f32[4096]{0:T(1024)} %param.7) | copy-start | bytes 49156
  46.1 3.4 copy-start.1
  49.6 12.9 %copy-start.4 = (f32[3,3,512]{2,1,0:T(4,128)S(1)}, f32[3,3,512]{2,1,0:T(4,128)}, u32[]{:S(2)}) copy-start(f32[3,3,512]{2,1,0:T(4,128)} %param.9) | copy-start | bytes 55300
  59.0 3.6 copy-start.3
  59.0 4.8 collective-permute-start
  68.7 1.2 copy-start.2
  290.3 8.2 copy-start
  326.1 186.9 %all-to-all-start.1 = ((f32[2,2,8,64,1024]{4,3,1,0,2:T(8,128)}), f32[2,2,8,64,1024]{4,3,1,0,2:T(8,128)}, u32[]{:S(2)}, u32[]{:S(2)}) async-start(f32[2,2,8,64,1024]{4,3,1,0,2:T(8,128)} %copy.60), calls=%async_computation.1 | async-start | bytes 16777216 | tf_op jit(solution)/shard_map/all_to_all | solution.py:44
  849.0 0.7 copy-start.5
Sparse Core Ops, SparseCore 0:
  8.9 37.1 all-gather.1
where the time goes:
time: 865 us; the launch traced here: 859 us
  blocking collectives  382 us (44%)
  waiting for transfers between devices  205 us (24%)
  matrix products  162 us (19%)
  local copies, waits for them, and re-layouts  66.5 us (8%)
  other arithmetic  19.3 us (2%)
  between operations  14.4 us (2%)
    all_to_all x2, blocking collectives, transposed(): lax.all_to_all(sectioned, 'context', split_axis=3, concat_axis=2, tiled=T...  286 us
    all_to_all x1, waiting for transfers between devices, transposed(): lax.all_to_all(combine_rows(lax.all_to_all(sectioned, 'context', split_ax...  182 us
    dot_general x8, matrix products, along_rows(): jnp.einsum('kj,tjc->tkc', table, block, precision=lax.Precision.HIGHEST)  108 us
    all_to_all x1, blocking collectives, transposed(): lax.all_to_all(combine_rows(lax.all_to_all(sectioned, 'context', split_ax...  96.5 us
    unnamed x21, local copies, waits for them, and re-layouts  24.8 us
    all_gather x1, waiting for transfers between devices, local(): lax.all_gather(tokens, 'tensor', axis=0, tiled=True).astype(jnp.float32)  21.8 us
  transfers between devices with their start and end apart: 3, of which 3 were waited for; matrix products, arithmetic and copies ran while one was open for 2% of the time, Pallas kernels for 0%

commit v1 on v0

--- a/solution.py
+++ b/solution.py
@@ -5,6 +5,27 @@
 from jax.sharding import PartitionSpec as P
 
 eps = 1e-06
+
+
+def collect(x, axis, dim):
+    size, position, rows = (lax.axis_size(axis), lax.axis_index(axis), x.shape[dim])
+    right = [(i, (i + 1) % size) for i in range(size)]
+    left = [(i, (i - 1) % size) for i in range(size)]
+    whole = jnp.zeros((*x.shape[:dim], size * rows, *x.shape[dim + 1 :]), x.dtype)
+    whole = lax.dynamic_update_slice_in_dim(whole, x, position * rows, axis=dim)
+    from_left = from_right = x
+    middle = size // 2
+    for hop in range(1, middle + 1):
+        from_left = lax.ppermute(from_left, axis, right)
+        whole = lax.dynamic_update_slice_in_dim(
+            whole, from_left, (position - hop) % size * rows, axis=dim
+        )
+        if hop < size - middle:
+            from_right = lax.ppermute(from_right, axis, left)
+            whole = lax.dynamic_update_slice_in_dim(
+                whole, from_right, (position + hop) % size * rows, axis=dim
+            )
+    return whole
 
 
 def shifted(x, axis, by):
@@ -68,7 +89,7 @@
     channels = in_weight.shape[2]
     tap_count = short_weight.shape[0]
     flat_weight = in_weight.reshape(width, 3 * channels)
-    values = lax.all_gather(tokens, "tensor", axis=0, tiled=True).astype(jnp.float32)
+    values = collect(tokens, "tensor", 0).astype(jnp.float32)
     inv_rms = lax.rsqrt(jnp.mean(values * values, axis=1, keepdims=True) + eps)
     normed = (values * inv_rms * norm_gain).astype(jnp.bfloat16)
     projected = jnp.dot(normed, flat_weight, preferred_element_type=jnp.float32)

time: 865 us -> 870 us (level)
  between operations: 14.4 us -> 0.99 us
  local copies, waits for them, and re-layouts: 66.5 us -> 75.8 us
    all_gather x1 -> x0, waiting for transfers between devices: 21.8 us -> none  [local(): lax.all_gather(tokens, 'tensor', axis=0, tiled=True).astype(jnp.float32)]
    ppermute x0 -> x3, waiting for transfers between devices: none -> 21.4 us  [the longest x2 21.4 us: collect(): from_left = lax.ppermute(from_left, axis, right)]
  transfers between devices with their start and end apart: 3 -> 5, of which waited for: 3 -> 3; matrix products, arithmetic and copies ran while one was open for 2% -> 3% of each run, Pallas kernels for 0% -> 0%
where the time goes in v1:
time: 870 us; the launch traced here: 863 us
  blocking collectives  385 us (44%)
  waiting for transfers between devices  206 us (24%)
  matrix products  164 us (19%)
  local copies, waits for them, and re-layouts  75.8 us (9%)
  other arithmetic  19.1 us (2%)
  starting transfers between devices  12.6 us (1%)
    all_to_all x2, blocking collectives, transposed(): lax.all_to_all(sectioned, 'context', split_axis=3, concat_axis=2, tiled=T...  288 us
    all_to_all x1, waiting for transfers between devices, transposed(): lax.all_to_all(combine_rows(lax.all_to_all(sectioned, 'context', split_ax...  183 us
    dot_general x8, matrix products, along_rows(): jnp.einsum('kj,tjc->tkc', table, block, precision=lax.Precision.HIGHEST)  108 us
    all_to_all x1, blocking collectives, transposed(): lax.all_to_all(combine_rows(lax.all_to_all(sectioned, 'context', split_ax...  96.5 us
    unnamed x21, local copies, waits for them, and re-layouts  26.1 us
    ppermute x2, waiting for transfers between devices, collect(): from_left = lax.ppermute(from_left, axis, right)  21.4 us
  transfers between devices with their start and end apart: 5, of which 3 were waited for; matrix products, arithmetic and copies ran while one was open for 3% of the time, Pallas kernels for 0%

profile of v1, /device:TPU:0, one launch (start us, length us, event | category | flops | bytes accessed | tf_op | source)
XLA Modules:
  0.0 862.8 jit_solution(14150730340586872842)
XLA Ops:
  2.4 21.4 %collective-permute-done = bf16[128,4096]{1,0:T(8,128)(2,1)S(1)} collective-permute-done((bf16[128,4096]{1,0:T(8,128)(2,1)}, bf16[128,4096]{1,0:T(8,128)(2,1)S(1)}, u32[]{:S(2)}, u32[]{:S(2)}) %collective-permute-start) | collective-permute-done | bytes 1048608 | tf_op jit(solution)/shard_map/ppermute | solution.py:19
  29.8 17.0 %copy.52 = bf16[4096,3,512]{0,2,1:T(8,128)(2,1)} copy(bf16[4096,3,512]{2,0,1:T(8,128)(2,1)} %param.8) | data formatting | bytes 25165824 | tf_op args[2]
  54.3 10.7 %fusion.3 = f32[512,1536]{1,0:T(8,128)S(1)} fusion(bf16[4096,1536]{0,1:T(8,128)(2,1)} %bitcast.124, bf16[512,4096]{1,0:T(8,128)(2,1)} %constant_dynamic-update-slice_fusion, f32[4096]{0:T(1024)S(1)} %copy-done.6, f32[512]{0:T(512)S(1)} %add_rsqrt_fusion), kind=kOutput, calls=%fused_computation.7 | convolution fusion | flops 6450839552 | bytes 19941376 | tf_op jit(solution)/shard_map/dot_general | solution.py:95
  80.0 7.4 copy.53
  87.4 191.4 %all_to_all.16 = f32[2,2,1,512,1024]{4,1,0,2,3:T(2,128)} all-to-all(f32[2,2,1,512,1024]{4,1,0,2,3:T(2,128)S(1)} %copy.53), channel_id=1, replica_groups=mesh['context'=8,'tensor'=4] {'context'}, dimensions={3} | all-to-all | bytes 16777216 | tf_op jit(solution)/shard_map/all_to_all | solution.py:67
  278.8 9.6 %fusion.167 = (f32[1,2,1,512,1024]{4,1,0,2,3:T(2,128)}, f32[1,2,1,512,1024]{4,1,0,2,3:T(2,128)}) fusion(f32[2,2,1,512,1024]{4,1,0,2,3:T(2,128)} %all_to_all.16), kind=kLoop, calls=%fused_computation.189 | loop fusion | bytes 16777216 | tf_op jit(solution)/shard_map/slice | solution.py:56
  291.9 7.8 fusion.9
  299.7 8.1 fusion.7
  309.2 8.1 subtract_bitcast_fusion.1
  317.4 8.0 add_bitcast_fusion.1
  327.0 8.5 copy.60
  335.5 5.0 all-to-all-start.1
  340.6 183.4 %all-to-all-done.1 = f32[2,2,8,64,1024]{4,3,1,0,2:T(8,128)} async-done(((f32[2,2,8,64,1024]{4,3,1,0,2:T(8,128)}), f32[2,2,8,64,1024]{4,3,1,0,2:T(8,128)}, u32[]{:S(2)}, u32[]{:S(2)}) %all-to-all-start.1) | async-done | bytes 8388640 | tf_op jit(solution)/shard_map/all_to_all | solution.py:65
  529.4 18.1 %fusion.37 = f32[2,1024,512]{2,1,0:T(8,128)S(1)} fusion(f32[2,512,1024]{2,1,0:T(8,128)S(1)} %bitcast.111, f32[2,512,1024]{2,1,0:T(8,128)S(1)} %bitcast.107, f32[2,512]{1,0:T(2,128)S(1)} %get-tuple-element.21, f32[2,512]{1,0:T(2,128)S(1)} %get-tuple-element.20), kind=kOutput, calls=%fused_computation.59 | convolution fusion | flops 6449266688 | bytes 12591104 | tf_op jit(solution)/shard_map/kj,tjc->tkc/dot_general | solution.py:38
  547.5 18.5 %fusion.38 = f32[2,1024,512]{2,1,0:T(8,128)S(1)} fusion(f32[2,512,1024]{2,1,0:T(8,128)S(1)} %bitcast.112, f32[2,512,1024]{2,1,0:T(8,128)S(1)} %bitcast.108, f32[2,512]{1,0:T(2,128)S(1)} %get-tuple-element.21, f32[2,512]{1,0:T(2,128)S(1)} %get-tuple-element.20), kind=kOutput, calls=%fused_computation.60 | convolution fusion | flops 6449266688 | bytes 12591104 | tf_op jit(solution)/shard_map/kj,tjc->tkc/dot_general | solution.py:38
  566.0 18.2 %add_bitcast_fusion = f32[2,512,1024]{1,2,0:T(8,128)S(1)} fusion(f32[2,1024,512]{2,1,0:T(8,128)S(1)} %fusion.37, f32[2,512,1024]{2,1,0:T(8,128)S(1)} %bitcast.113, f32[2,512,1024]{2,1,0:T(8,128)S(1)} %bitcast.109, f32[2,512]{1,0:T(2,128)S(1)} %get-tuple-element.21, f32[2,512]{1,0:T(2,128)S(1)} %get-tuple-element.20), kind=kOutput, calls=%fused_computation.12 | convolution fusion | flops 6450315264 | bytes 16785408 | tf_op jit(solution)/shard_map/kj,tjc->tkc/dot_general | solution.py:38
  584.2 18.6 %subtract_bitcast_fusion = f32[2,512,1024]{1,2,0:T(8,128)S(1)} fusion(f32[2,1024,512]{2,1,0:T(8,128)S(1)} %fusion.38, f32[2,512,1024]{2,1,0:T(8,128)S(1)} %bitcast.114, f32[2,512,1024]{2,1,0:T(8,128)S(1)} %bitcast.110, f32[2,512]{1,0:T(2,128)S(1)} %get-tuple-element.21, f32[2,512]{1,0:T(2,128)S(1)} %get-tuple-element.20), kind=kOutput, calls=%fused_computation.11 | convolution fusion | flops 6450315264 | bytes 16785408 | tf_op jit(solution)/shard_map/kj,tjc->tkc/dot_general | solution.py:38
  604.1 8.4 fusion.49
  612.6 8.4 fusion.55
  621.0 8.6 convolution_add_fusion
  629.6 8.7 %add_bitcast_fusion.3 = (f32[1,2,512,512]{2,3,1,0:T(8,128)S(1)}, f32[1,2,512,512]{2,3,1,0:T(8,128)S(1)}) fusion(f32[2,512,512]{2,1,0:T(8,128)S(1)} %convolution_add_fusion, f32[2,512]{1,0:T(2,128)S(1)} %get-tuple-element.21, f32[2,512]{1,0:T(2,128)S(1)} %get-tuple-element.20, f32[2,512,512]{2,1,0:T(8,128)S(1)} %fusion.55, ...), kind=kOutput, calls=%fused_computation.41 | convolution fusion | flops 3228565504 | bytes 10493952 | tf_op jit(solution)/shard_map/kj,tjc->tkc/dot_general | solution.py:38
  640.7 7.3 copy.67
  648.0 96.9 %all_to_all.17 = f32[2,2,1,512,512]{4,1,0,2,3:T(2,128)S(1)} all-to-all(f32[2,2,1,512,512]{4,1,0,2,3:T(2,128)} %copy.67), channel_id=1, replica_groups=mesh['context'=8,'tensor'=4] {'context'}, dimensions={3} | all-to-all | bytes 8388608 | tf_op jit(solution)/shard_map/all_to_all | solution.py:77
  763.5 96.5 %all_to_all.18 = f32[2,2,8,64,512]{4,3,1,0,2:T(8,128)S(1)} all-to-all(f32[2,2,8,64,512]{4,3,1,0,2:T(8,128)S(1)} %copy.74), channel_id=1, replica_groups=mesh['context'=8,'tensor'=4] {'context'}, dimensions={2} | all-to-all | bytes 8388608 | tf_op jit(solution)/shard_map/all_to_all | solution.py:75
  (61 shorter events, 67.3 us)
Async XLA Ops:
  0.0 28.7 %copy-start.3 = (bf16[128,4096]{1,0:T(8,128)(2,1)S(1)}, bf16[128,4096]{1,0:T(8,128)(2,1)}, u32[]{:S(2)}) copy-start(bf16[128,4096]{1,0:T(8,128)(2,1)} %param.6) | copy-start | bytes 3145732
  0.0 23.8 %collective-permute-start = (bf16[128,4096]{1,0:T(8,128)(2,1)}, bf16[128,4096]{1,0:T(8,128)(2,1)S(1)}, u32[]{:S(2)}, u32[]{:S(2)}) collective-permute-start(bf16[128,4096]{1,0:T(8,128)(2,1)} %param.6), channel_id=1, source_target_pairs={{0,1},{1,2},{2,3},{3,0},{4,5},{5,6},{6,7},{7,4},{8,9},{9,10},{10,1... | collective-permute-start | bytes 3145736 | tf_op jit(solution)/shard_map/ppermute | solution.py:19
  0.5 47.4 %collective-permute-start.1 = (bf16[128,4096]{1,0:T(8,128)(2,1)}, bf16[128,4096]{1,0:T(8,128)(2,1)S(1)}, u32[]{:S(2)}, u32[]{:S(2)}) collective-permute-start(bf16[128,4096]{1,0:T(8,128)(2,1)} %param.6), channel_id=1, source_target_pairs={{0,3},{1,0},{2,1},{3,2},{4,7},{5,4},{6,5},{7,6},{8,11},{9,8},{10,9... | collective-permute-start | bytes 3145736 | tf_op jit(solution)/shard_map/ppermute | solution.py:24
  23.8 25.1 %collective-permute-start.2 = (bf16[128,4096]{1,0:T(8,128)(2,1)S(1)}, bf16[128,4096]{1,0:T(8,128)(2,1)}, u32[]{:S(2)}, u32[]{:S(2)}) collective-permute-start(bf16[128,4096]{1,0:T(8,128)(2,1)S(1)} %collective-permute-done), channel_id=1, source_target_pairs={{0,1},{1,2},{2,3},{3,0},{4,5},{5,6},{6,7},{7,4},{8,9},{9,10},{10,1... | collective-permute-start | bytes 3145736 | tf_op jit(solution)/shard_map/ppermute | solution.py:19
  47.8 6.4 copy-start.6
  54.3 15.0 %copy-start.4 = (f32[3,3,512]{2,1,0:T(4,128)S(1)}, f32[3,3,512]{2,1,0:T(4,128)}, u32[]{:S(2)}) copy-start(f32[3,3,512]{2,1,0:T(4,128)} %param.9) | copy-start | bytes 55300
  64.9 1.6 copy-start.2
  66.6 4.1 collective-permute-start.3
  75.6 1.2 copy-start.1
  299.7 8.2 copy-start
  335.5 188.5 %all-to-all-start.1 = ((f32[2,2,8,64,1024]{4,3,1,0,2:T(8,128)}), f32[2,2,8,64,1024]{4,3,1,0,2:T(8,128)}, u32[]{:S(2)}, u32[]{:S(2)}) async-start(f32[2,2,8,64,1024]{4,3,1,0,2:T(8,128)} %copy.60), calls=%async_computation.1 | async-start | bytes 16777216 | tf_op jit(solution)/shard_map/all_to_all | solution.py:65
  860.0 0.7 copy-start.5
